TPU v7x, 128 devices: a whole 4x4x4 slice. The times are simulated.
128 devices in a mesh: row: 8 (over z, x_lo), col: 16 (over x_hi, y, core).
Axes of the slice: x: 4 (x_hi: 2, x_lo: 2; x = x_hi * 2 + x_lo), y: 4, z: 4, core: 2. Of those that a mesh axis runs over, the one named last changes fastest.
Arguments:
- stream: float32 [16384, 256], P(('row', 'col')), may hold values from -130 to 130
- stream_tail: float32 [31, 256], replicated, may hold values from -130 to 130
- archive: float32 [65536, 256], P(('col', 'row')), may hold values from -60 to 60
- archive_tail: float32 [31, 256], replicated, may hold values from -60 to 60
Outputs:
- row_profile: float32 [16384], P(('row', 'col'))
- col_profile: float32 [65536], P(('col', 'row'))
All inputs are finite; a program needn't handle non-finite values.
Results may differ from a plain program's by a relative error of at most 0.0003.
Values sent between devices are 32-bit elements; how exact they have to be, the bound alone decides.
A program may use at most 128 MiB of HBM per device.

v0:
```python
import jax
import jax.numpy as jnp
from jax import lax
from jax.sharding import PartitionSpec as P

M = 32


def from_behind(block, axis, distance):
    devices = range(lax.axis_size(axis))
    route = [((i - distance) % len(devices), i) for i in devices]
    return lax.ppermute(block, axis, route)


def shifted(value, axis, steps):
    count = lax.axis_size(axis)
    leading, last = (max(0, -steps), min(count, count - steps))
    return lax.ppermute(value, axis, [(source, source + steps) for source in range(leading, last)])


def to_unit(frames):
    return frames / jnp.sqrt(jnp.sum(frames * frames, axis=1, keepdims=True) + 1e-06)


def window_sum(gram_block):
    summed = gram_block
    width = 1
    while width < M:
        height = summed.shape[0] - width
        breadth = summed.shape[1] - width
        summed = summed[0:height, 0:breadth] + summed[width:, width:]
        width = width * 2
    return summed


def profile_tile(stream_ext, archive_ext):
    row_count = stream_ext.shape[0] - (M - 1)
    col_count = archive_ext.shape[0] - (M - 1)
    block_rows = min(256, row_count)
    while block_rows * col_count < 2**20 and row_count % (block_rows * 2) == 0:
        block_rows = block_rows * 2
    steps_count = row_count // block_rows

    def advance(col_best, position):
        first_row = position * block_rows
        window_rows = lax.dynamic_slice_in_dim(stream_ext, first_row, block_rows + M - 1, 0)
        gram_block = lax.dot_general(
            window_rows,
            archive_ext,
            (((1,), (1,)), ((), ())),
            precision=lax.Precision.HIGHEST,
            preferred_element_type=jnp.float32,
        )
        scores = window_sum(gram_block) / M
        return (jnp.maximum(col_best, jnp.max(scores, axis=0)), jnp.max(scores, axis=1))

    start_best = jnp.full((col_count,), -2.0, jnp.float32)
    col_best, row_best = lax.scan(advance, start_best, jnp.arange(steps_count, dtype=jnp.int32))
    return (row_best.reshape(-1), col_best)


def on_device(stream, stream_tail, archive, archive_tail):
    stream_unit = to_unit(stream)
    archive_unit = to_unit(archive)
    stream_after = to_unit(stream_tail)
    archive_after = to_unit(archive_tail)
    last_row = lax.axis_index("row") == lax.axis_size("row") - 1
    last_col = lax.axis_index("col") == lax.axis_size("col") - 1
    stream_all = lax.all_gather(stream_unit, ("row", "col"), axis=0, tiled=True)
    stream_ext = jnp.concatenate([stream_all, stream_after], axis=0)
    head_rows = archive_unit[: M - 1]
    from_below = from_behind(head_rows, "row", -1)
    from_beside = shifted(from_below, "col", -1)
    following = jnp.where(last_row, jnp.where(last_col, archive_after, from_beside), from_below)
    archive_ext = jnp.concatenate([archive_unit, following], axis=0)
    row_best, col_profile = profile_tile(stream_ext, archive_ext)
    row_best = lax.pmax(row_best, ("row", "col"))
    own_len = stream.shape[0]
    flat_index = lax.axis_index("row") * lax.axis_size("col") + lax.axis_index("col")
    row_profile = lax.dynamic_slice_in_dim(row_best, flat_index * own_len, own_len)
    return (row_profile, col_profile)


def solution(mesh):
    return jax.shard_map(
        on_device,
        mesh=mesh,
        in_specs=(P(("row", "col"), None), P(), P(("col", "row"), None), P()),
        out_specs=(P(("row", "col")), P(("col", "row"))),
        check_vma=False,
    )
```

profile of v0, /device:TPU:1, one launch (start us, length us, event | category | flops | bytes accessed | tf_op | source)
XLA Modules:
  0.0 509.9 jit_solution(15961827501369002649)
XLA Ops:
  8.2 1.6 broadcast_divide_fusion.1
  12.4 5.6 %collective-permute-start = (f32[31,256]{1,0:T(8,128)S(1)}, f32[31,256]{1,0:T(8,128)S(1)}, u32[]{:S(2)}, u32[]{:S(2)}) collective-permute-start(f32[31,256]{1,0:T(8,128)S(1)} %slice.54), channel_id=1, source_target_pairs={{16,0},{32,16},{48,32},{64,48},{80,64},{96,80},{112,96},{0,112},{1... | collective-permute-start | bytes 95240 | tf_op jit(solution)/shard_map/ppermute | solution.py:12
  20.5 2.9 collective-permute-start.1
  23.4 2.8 collective-permute-done.1
  27.1 197.7 %all-gather.2.cloned.1.call-done = f32[16384,256]{1,0:T(8,128)} async-done(((f32[128,256]{1,0:T(8,128)}), f32[16384,256]{1,0:T(8,128)}) %all-gather.2.cloned.1.call-update) | async-done | bytes 16777232 | tf_op jit(solution)/shard_map/all_gather | solution.py:69
  224.8 14.4 %pad_maximum_fusion = f32[16415,256]{1,0:T(8,128)} fusion(f32[31,256]{1,0:T(8,128)S(1)} %broadcast_divide_fusion.2, f32[16384,256]{1,0:T(8,128)} %all-gather.2.cloned.1.call-done), kind=kLoop, calls=%fused_computation.12 | loop fusion | flops 4202240 | bytes 33617920 | tf_op jit(solution)/shard_map/concatenate | solution.py:70
  239.2 123.0 %while.13 = (s32[]{:T(128)}, f32[512]{0:T(512)S(1)}, f32[8,2048]{1,0:T(8,128)S(1)}, s32[8]{0:T(128)S(1)}, f32[16415,256]{1,0:T(8,128)}, /*index=5*/f32[543,256]{...) while((s32[]{:T(128)}, f32[512]{0:T(512)S(1)}, f32[8,2048]{1,0:T(8,128)S(1)}, ...), condition=%wide.region_7.8_spmd.clone, body=%wide.region_4.7_spmd.clone.sunk | while | flops 3476612096 | bytes 68995496 | solution.py:58
  240.5 6.3 %fusion.13 = f32[2079,543]{0,1:T(8,128)S(1)} fusion(f32[543,256]{1,0:T(8,128)S(1)} %get-tuple-element.138, f32[16415,256]{1,0:T(8,128)} %get-tuple-element.137, s32[]{:T(128)S(6)} %select_n.31), kind=kOutput, calls=%fused_computation.6.clone.1 | convolution fusion | flops 3467971584 | bytes 7201544 | tf_op jit(solution)/shard_map/while/body/eval_jaxpr/dot_general | solution.py:47
  246.8 1.7 slice_add_fusion.9
  248.5 1.7 slice_add_fusion.10
  255.9 6.3 %fusion.13 = f32[2079,543]{0,1:T(8,128)S(1)} fusion(f32[543,256]{1,0:T(8,128)S(1)} %get-tuple-element.138, f32[16415,256]{1,0:T(8,128)} %get-tuple-element.137, s32[]{:T(128)S(6)} %select_n.31), kind=kOutput, calls=%fused_computation.6.clone.1 | convolution fusion | flops 3467971584 | bytes 7201544 | tf_op jit(solution)/shard_map/while/body/eval_jaxpr/dot_general | solution.py:47
  262.2 1.7 slice_add_fusion.9
  263.9 1.7 slice_add_fusion.10
  271.3 6.3 %fusion.13 = f32[2079,543]{0,1:T(8,128)S(1)} fusion(f32[543,256]{1,0:T(8,128)S(1)} %get-tuple-element.138, f32[16415,256]{1,0:T(8,128)} %get-tuple-element.137, s32[]{:T(128)S(6)} %select_n.31), kind=kOutput, calls=%fused_computation.6.clone.1 | convolution fusion | flops 3467971584 | bytes 7201544 | tf_op jit(solution)/shard_map/while/body/eval_jaxpr/dot_general | solution.py:47
  277.6 1.7 slice_add_fusion.9
  279.3 1.7 slice_add_fusion.10
  286.6 6.3 %fusion.13 = f32[2079,543]{0,1:T(8,128)S(1)} fusion(f32[543,256]{1,0:T(8,128)S(1)} %get-tuple-element.138, f32[16415,256]{1,0:T(8,128)} %get-tuple-element.137, s32[]{:T(128)S(6)} %select_n.31), kind=kOutput, calls=%fused_computation.6.clone.1 | convolution fusion | flops 3467971584 | bytes 7201544 | tf_op jit(solution)/shard_map/while/body/eval_jaxpr/dot_general | solution.py:47
  293.0 1.7 slice_add_fusion.9
  294.6 1.7 slice_add_fusion.10
  302.0 6.3 %fusion.13 = f32[2079,543]{0,1:T(8,128)S(1)} fusion(f32[543,256]{1,0:T(8,128)S(1)} %get-tuple-element.138, f32[16415,256]{1,0:T(8,128)} %get-tuple-element.137, s32[]{:T(128)S(6)} %select_n.31), kind=kOutput, calls=%fused_computation.6.clone.1 | convolution fusion | flops 3467971584 | bytes 7201544 | tf_op jit(solution)/shard_map/while/body/eval_jaxpr/dot_general | solution.py:47
  308.4 1.7 slice_add_fusion.9
  310.0 1.7 slice_add_fusion.10
  317.4 6.3 %fusion.13 = f32[2079,543]{0,1:T(8,128)S(1)} fusion(f32[543,256]{1,0:T(8,128)S(1)} %get-tuple-element.138, f32[16415,256]{1,0:T(8,128)} %get-tuple-element.137, s32[]{:T(128)S(6)} %select_n.31), kind=kOutput, calls=%fused_computation.6.clone.1 | convolution fusion | flops 3467971584 | bytes 7201544 | tf_op jit(solution)/shard_map/while/body/eval_jaxpr/dot_general | solution.py:47
  323.7 1.7 slice_add_fusion.9
  325.4 1.7 slice_add_fusion.10
  332.8 6.3 %fusion.13 = f32[2079,543]{0,1:T(8,128)S(1)} fusion(f32[543,256]{1,0:T(8,128)S(1)} %get-tuple-element.138, f32[16415,256]{1,0:T(8,128)} %get-tuple-element.137, s32[]{:T(128)S(6)} %select_n.31), kind=kOutput, calls=%fused_computation.6.clone.1 | convolution fusion | flops 3467971584 | bytes 7201544 | tf_op jit(solution)/shard_map/while/body/eval_jaxpr/dot_general | solution.py:47
  339.1 1.7 slice_add_fusion.9
  340.8 1.7 slice_add_fusion.10
  348.2 6.3 %fusion.13 = f32[2079,543]{0,1:T(8,128)S(1)} fusion(f32[543,256]{1,0:T(8,128)S(1)} %get-tuple-element.138, f32[16415,256]{1,0:T(8,128)} %get-tuple-element.137, s32[]{:T(128)S(6)} %select_n.31), kind=kOutput, calls=%fused_computation.6.clone.1 | convolution fusion | flops 3467971584 | bytes 7201544 | tf_op jit(solution)/shard_map/while/body/eval_jaxpr/dot_general | solution.py:47
  354.5 1.7 slice_add_fusion.9
  356.2 1.7 slice_add_fusion.10
  363.0 138.8 %all-reduce.2.cloned.1.call-done = f32[16384]{0:T(1024)} async-done(((f32[16384]{0:T(1024)}), f32[16384]{0:T(1024)}) %all-reduce.2.cloned.1.call-update) | async-done | bytes 65552 | tf_op jit(solution)/shard_map/pmax | solution.py:77
  (73 shorter events, 48.9 us)
Async XLA Ops:
  7.2 217.6 %all-gather.2.cloned.1.call-start = ((), (), s32[]{:S(2)}) async-start(), calls=%async_computation | async-start | bytes 16908288 | tf_op jit(solution)/shard_map/all_gather | solution.py:69
  9.9 491.9 %all-reduce.2.cloned.1.call-start = ((), (), s32[]{:S(2)}) async-start(), calls=%async_computation.1 | async-start | bytes 131072 | tf_op jit(solution)/shard_map/pmax | solution.py:77
  12.4 8.2 %collective-permute-start = (f32[31,256]{1,0:T(8,128)S(1)}, f32[31,256]{1,0:T(8,128)S(1)}, u32[]{:S(2)}, u32[]{:S(2)}) collective-permute-start(f32[31,256]{1,0:T(8,128)S(1)} %slice.54), channel_id=1, source_target_pairs={{16,0},{32,16},{48,32},{64,48},{80,64},{96,80},{112,96},{0,112},{1... | collective-permute-start | bytes 95240 | tf_op jit(solution)/shard_map/ppermute | solution.py:12
  20.5 5.7 %collective-permute-start.1 = (f32[31,256]{1,0:T(8,128)S(1)}, f32[31,256]{1,0:T(8,128)S(1)}, u32[]{:S(2)}, u32[]{:S(2)}) collective-permute-start(f32[31,256]{1,0:T(8,128)S(1)} %collective-permute-done), channel_id=1, source_target_pairs={{1,0},{2,1},{3,2},{4,3},{5,4},{6,5},{7,6},{8,7},{9,8},{10,9},{11,1... | collective-permute-start | bytes 95240 | tf_op jit(solution)/shard_map/ppermute | solution.py:18
  362.3 140.8 %copy-start = (f32[512]{0:T(512)}, f32[512]{0:T(512)S(1)}, u32[]{:S(2)}) copy-start(f32[512]{0:T(512)S(1)} %get-tuple-element.34) | copy-start | bytes 6148
Sparse Core Ops, SparseCore 0:
  10.0 214.7 all-gather.1
  363.1 138.6 all-reduce.1
where the time goes:
time: 511 us; the launch traced here: 510 us
  waiting for transfers between devices  339 us (66%)
  other arithmetic  83.3 us (16%)
  matrix products  50.6 us (10%)
  between operations  14.2 us (3%)
  starting transfers between devices  8.51 us (2%)
  local copies, waits for them, and re-layouts  8.22 us (2%)
  loops' own time  5.71 us (1%)
    all_gather x1, waiting for transfers between devices, on_device(): stream_all = lax.all_gather(stream_unit, ('row', 'col'), axis=0, tiled=True)  198 us
    pmax x1, waiting for transfers between devices, on_device(): row_best = lax.pmax(row_best, ('row', 'col'))  139 us
    dot_general x8, matrix products, advance(): lax.dot_general(window_rows, archive_ext, (((1,), (1,)), ((), ())), preci...  50.6 us
    add x32, other arithmetic, window_sum(): summed = summed[0:height, 0:breadth] + summed[width:, width:]  49.6 us
    concatenate x1, other arithmetic, on_device(): stream_ext = jnp.concatenate([stream_all, stream_after], axis=0)  14.4 us
    reduce_max x8, other arithmetic, advance(): jnp.max(scores, axis=1)  10.6 us
  transfers between devices with their start and end apart: 4, of which 3 were waited for; matrix products, arithmetic and copies ran while one was open for 1% of the time, Pallas kernels for 0%

commit v1 on v0

--- a/solution.py
+++ b/solution.py
@@ -66,7 +66,12 @@
     archive_after = to_unit(archive_tail)
     last_row = lax.axis_index("row") == lax.axis_size("row") - 1
     last_col = lax.axis_index("col") == lax.axis_size("col") - 1
-    stream_all = lax.all_gather(stream_unit, ("row", "col"), axis=0, tiled=True)
+    stream_all = jnp.concatenate(
+        lax.all_to_all(
+            jnp.stack([stream_unit] * lax.axis_size(("row", "col"))), ("row", "col"), 0, 0
+        ),
+        axis=0,
+    )
     stream_ext = jnp.concatenate([stream_all, stream_after], axis=0)
     head_rows = archive_unit[: M - 1]
     from_below = from_behind(head_rows, "row", -1)

time: 511 us -> 542 us (1.061)
  waiting for transfers between devices: 339 us -> 358 us
  starting transfers between devices: 8.51 us -> 19 us
  local copies, waits for them, and re-layouts: 8.22 us -> 16 us
  other arithmetic: 83.3 us -> 77.5 us
    ppermute x1, waiting for transfers between devices: 0.01 us -> 198 us  [from_behind(): return lax.ppermute(block, axis, route)]
    all_gather x1 -> x0, waiting for transfers between devices: 198 us -> none  [on_device(): stream_all = lax.all_gather(stream_unit, ('row', 'col'), axis=0, tiled=True)]
    all_to_all x0 -> x1, starting transfers between devices: none -> 11.9 us  [on_device(): lax.all_to_all(jnp.stack([stream_unit] * lax.axis_size(('row', 'col'))),...]
    pmax x1, waiting for transfers between devices: 139 us -> 147 us  [on_device(): row_best = lax.pmax(row_best, ('row', 'col'))]
    another operation x0 -> x1, local copies, waits for them, and re-layouts: none -> 7.8 us  [on_device(): jnp.stack([stream_unit] * lax.axis_size(('row', 'col')))]
    all_to_all x0 -> x1, waiting for transfers between devices: none -> 6.86 us  [on_device(): lax.all_to_all(jnp.stack([stream_unit] * lax.axis_size(('row', 'col'))),...]
  transfers between devices with their start and end apart: 4 -> 4, of which waited for: 3 -> 4; matrix products, arithmetic and copies ran while one was open for 1% -> 0% of each run, Pallas kernels for 0% -> 0%
where the time goes in v1:
time: 542 us
  waiting for transfers between devices  358 us (66%)
  other arithmetic  77.5 us (14%)
  matrix products  50.6 us (9%)
  starting transfers between devices  19 us (4%)
  local copies, waits for them, and re-layouts  16 us (3%)
  between operations  14.2 us (3%)
  loops' own time  5.71 us (1%)
    ppermute x1, waiting for transfers between devices, from_behind(): return lax.ppermute(block, axis, route)  198 us
    pmax x1, waiting for transfers between devices, on_device(): row_best = lax.pmax(row_best, ('row', 'col'))  147 us
    dot_general x8, matrix products, advance(): lax.dot_general(window_rows, archive_ext, (((1,), (1,)), ((), ())), preci...  50.6 us
    add x32, other arithmetic, window_sum(): summed = summed[0:height, 0:breadth] + summed[width:, width:]  49.6 us
    concatenate x1, other arithmetic, on_device(): stream_ext = jnp.concatenate([stream_all, stream_after], axis=0)  14.4 us
    all_to_all x1, starting transfers between devices, on_device(): lax.all_to_all(jnp.stack([stream_unit] * lax.axis_size(('row', 'col'))),...  11.9 us
  transfers between devices with their start and end apart: 4, of which 4 were waited for; matrix products, arithmetic and copies ran while one was open for 0% of the time, Pallas kernels for 0%

profile of v1, /device:TPU:1, one launch (start us, length us, event | category | flops | bytes accessed | tf_op | source)
XLA Modules:
  0.0 541.6 jit_solution(9242035947957610957)
XLA Ops:
  9.2 7.8 %stack.2 = f32[128,128,256]{2,1,0:T(8,128)} broadcast(f32[128,256]{1,0:T(8,128)S(1)} %broadcast_divide_fusion.1), dimensions={1,2} | broadcast | bytes 16908288 | tf_op jit(solution)/shard_map/stack | solution.py:71
  17.0 11.9 %all-to-all-start = ((f32[128,128,256]{2,1,0:T(8,128)}), f32[128,128,256]{2,1,0:T(8,128)}, u32[]{:S(2)}, u32[]{:S(2)}) async-start(f32[128,128,256]{2,1,0:T(8,128)} %stack.2), calls=%async_computation | async-start | bytes 33554432 | tf_op jit(solution)/shard_map/all_to_all | solution.py:70
  29.3 4.2 collective-permute-start
  33.9 198.2 %collective-permute-done = f32[31,256]{1,0:T(8,128)S(1)} collective-permute-done((f32[31,256]{1,0:T(8,128)S(1)}, f32[31,256]{1,0:T(8,128)S(1)}, u32[]{:S(2)}, u32[]{:S(2)}) %collective-permute-start) | collective-permute-done | bytes 31776 | tf_op jit(solution)/shard_map/ppermute | solution.py:12
  232.1 2.8 collective-permute-start.1
  234.9 6.0 %collective-permute-done.1 = f32[31,256]{1,0:T(8,128)S(1)} collective-permute-done((f32[31,256]{1,0:T(8,128)S(1)}, f32[31,256]{1,0:T(8,128)S(1)}, u32[]{:S(2)}, u32[]{:S(2)}) %collective-permute-start.1) | collective-permute-done | bytes 31776 | tf_op jit(solution)/shard_map/ppermute | solution.py:18
  241.0 6.9 %all-to-all-done = f32[128,128,256]{2,1,0:T(8,128)} async-done(((f32[128,128,256]{2,1,0:T(8,128)}), f32[128,128,256]{2,1,0:T(8,128)}, u32[]{:S(2)}, u32[]{:S(2)}) %all-to-all-start) | async-done | bytes 16777248 | tf_op jit(solution)/shard_map/all_to_all | solution.py:70
  247.9 14.4 %pad_maximum_fusion = f32[16415,256]{1,0:T(8,128)} fusion(f32[31,256]{1,0:T(8,128)S(1)} %broadcast_divide_fusion.2, f32[16384,256]{1,0:T(8,128)} %bitcast), kind=kLoop, calls=%fused_computation.12 | loop fusion | flops 4202240 | bytes 33617920 | tf_op jit(solution)/shard_map/concatenate | solution.py:75
  262.3 123.0 %while.13 = (s32[]{:T(128)}, f32[512]{0:T(512)S(1)}, f32[8,2048]{1,0:T(8,128)S(1)}, s32[8]{0:T(128)S(1)}, f32[16415,256]{1,0:T(8,128)}, /*index=5*/f32[543,256]{...) while((s32[]{:T(128)}, f32[512]{0:T(512)S(1)}, f32[8,2048]{1,0:T(8,128)S(1)}, ...), condition=%wide.region_7.8_spmd.clone, body=%wide.region_4.7_spmd.clone.sunk | while | flops 3476612096 | bytes 68995496 | solution.py:58
  263.6 6.3 %fusion.13 = f32[2079,543]{0,1:T(8,128)S(1)} fusion(f32[543,256]{1,0:T(8,128)S(1)} %get-tuple-element.138, f32[16415,256]{1,0:T(8,128)} %get-tuple-element.137, s32[]{:T(128)S(6)} %select_n.31), kind=kOutput, calls=%fused_computation.6.clone.1 | convolution fusion | flops 3467971584 | bytes 7201544 | tf_op jit(solution)/shard_map/while/body/eval_jaxpr/dot_general | solution.py:47
  269.9 1.7 slice_add_fusion.9
  271.6 1.7 slice_add_fusion.10
  279.0 6.3 %fusion.13 = f32[2079,543]{0,1:T(8,128)S(1)} fusion(f32[543,256]{1,0:T(8,128)S(1)} %get-tuple-element.138, f32[16415,256]{1,0:T(8,128)} %get-tuple-element.137, s32[]{:T(128)S(6)} %select_n.31), kind=kOutput, calls=%fused_computation.6.clone.1 | convolution fusion | flops 3467971584 | bytes 7201544 | tf_op jit(solution)/shard_map/while/body/eval_jaxpr/dot_general | solution.py:47
  285.3 1.7 slice_add_fusion.9
  287.0 1.7 slice_add_fusion.10
  294.3 6.3 %fusion.13 = f32[2079,543]{0,1:T(8,128)S(1)} fusion(f32[543,256]{1,0:T(8,128)S(1)} %get-tuple-element.138, f32[16415,256]{1,0:T(8,128)} %get-tuple-element.137, s32[]{:T(128)S(6)} %select_n.31), kind=kOutput, calls=%fused_computation.6.clone.1 | convolution fusion | flops 3467971584 | bytes 7201544 | tf_op jit(solution)/shard_map/while/body/eval_jaxpr/dot_general | solution.py:47
  300.7 1.7 slice_add_fusion.9
  302.4 1.7 slice_add_fusion.10
  309.7 6.3 %fusion.13 = f32[2079,543]{0,1:T(8,128)S(1)} fusion(f32[543,256]{1,0:T(8,128)S(1)} %get-tuple-element.138, f32[16415,256]{1,0:T(8,128)} %get-tuple-element.137, s32[]{:T(128)S(6)} %select_n.31), kind=kOutput, calls=%fused_computation.6.clone.1 | convolution fusion | flops 3467971584 | bytes 7201544 | tf_op jit(solution)/shard_map/while/body/eval_jaxpr/dot_general | solution.py:47
  316.1 1.7 slice_add_fusion.9
  317.7 1.7 slice_add_fusion.10
  325.1 6.3 %fusion.13 = f32[2079,543]{0,1:T(8,128)S(1)} fusion(f32[543,256]{1,0:T(8,128)S(1)} %get-tuple-element.138, f32[16415,256]{1,0:T(8,128)} %get-tuple-element.137, s32[]{:T(128)S(6)} %select_n.31), kind=kOutput, calls=%fused_computation.6.clone.1 | convolution fusion | flops 3467971584 | bytes 7201544 | tf_op jit(solution)/shard_map/while/body/eval_jaxpr/dot_general | solution.py:47
  331.4 1.7 slice_add_fusion.9
  333.1 1.7 slice_add_fusion.10
  340.5 6.3 %fusion.13 = f32[2079,543]{0,1:T(8,128)S(1)} fusion(f32[543,256]{1,0:T(8,128)S(1)} %get-tuple-element.138, f32[16415,256]{1,0:T(8,128)} %get-tuple-element.137, s32[]{:T(128)S(6)} %select_n.31), kind=kOutput, calls=%fused_computation.6.clone.1 | convolution fusion | flops 3467971584 | bytes 7201544 | tf_op jit(solution)/shard_map/while/body/eval_jaxpr/dot_general | solution.py:47
  346.8 1.7 slice_add_fusion.9
  348.5 1.7 slice_add_fusion.10
  355.9 6.3 %fusion.13 = f32[2079,543]{0,1:T(8,128)S(1)} fusion(f32[543,256]{1,0:T(8,128)S(1)} %get-tuple-element.138, f32[16415,256]{1,0:T(8,128)} %get-tuple-element.137, s32[]{:T(128)S(6)} %select_n.31), kind=kOutput, calls=%fused_computation.6.clone.1 | convolution fusion | flops 3467971584 | bytes 7201544 | tf_op jit(solution)/shard_map/while/body/eval_jaxpr/dot_general | solution.py:47
  362.2 1.7 slice_add_fusion.9
  371.3 6.3 %fusion.13 = f32[2079,543]{0,1:T(8,128)S(1)} fusion(f32[543,256]{1,0:T(8,128)S(1)} %get-tuple-element.138, f32[16415,256]{1,0:T(8,128)} %get-tuple-element.137, s32[]{:T(128)S(6)} %select_n.31), kind=kOutput, calls=%fused_computation.6.clone.1 | convolution fusion | flops 3467971584 | bytes 7201544 | tf_op jit(solution)/shard_map/while/body/eval_jaxpr/dot_general | solution.py:47
  379.3 1.7 slice_add_fusion.10
  386.1 147.4 %all-reduce.2.cloned.1.call-done = f32[16384]{0:T(1024)} async-done(((f32[16384]{0:T(1024)}), f32[16384]{0:T(1024)}) %all-reduce.2.cloned.1.call-update) | async-done | bytes 65552 | tf_op jit(solution)/shard_map/pmax | solution.py:82
  (79 shorter events, 48.0 us)
Async XLA Ops:
  17.0 12.0 %copy-start = (f32[512,256]{1,0:T(8,128)S(1)}, f32[512,256]{1,0:T(8,128)}, u32[]{:S(2)}) copy-start(f32[512,256]{1,0:T(8,128)} %param.8) | copy-start | bytes 1572868
  17.0 16.6 %copy-start.1 = (f32[31,256]{1,0:T(8,128)S(1)}, f32[31,256]{1,0:T(8,128)}, u32[]{:S(2)}) copy-start(f32[31,256]{1,0:T(8,128)} %param.7) | copy-start | bytes 95236
  17.0 16.8 %copy-start.2 = (f32[31,256]{1,0:T(8,128)S(1)}, f32[31,256]{1,0:T(8,128)}, u32[]{:S(2)}) copy-start(f32[31,256]{1,0:T(8,128)} %param.9) | copy-start | bytes 95236
  17.0 230.9 %all-to-all-start = ((f32[128,128,256]{2,1,0:T(8,128)}), f32[128,128,256]{2,1,0:T(8,128)}, u32[]{:S(2)}, u32[]{:S(2)}) async-start(f32[128,128,256]{2,1,0:T(8,128)} %stack.2), calls=%async_computation | async-start | bytes 33554432 | tf_op jit(solution)/shard_map/all_to_all | solution.py:70
  29.0 504.5 %all-reduce.2.cloned.1.call-start = ((), (), s32[]{:S(2)}) async-start(), calls=%async_computation.1 | async-start | bytes 131072 | tf_op jit(solution)/shard_map/pmax | solution.py:82
  29.3 202.7 %collective-permute-start = (f32[31,256]{1,0:T(8,128)S(1)}, f32[31,256]{1,0:T(8,128)S(1)}, u32[]{:S(2)}, u32[]{:S(2)}) collective-permute-start(f32[31,256]{1,0:T(8,128)S(1)} %slice.54), channel_id=1, source_target_pairs={{16,0},{32,16},{48,32},{64,48},{80,64},{96,80},{112,96},{0,112},{1... | collective-permute-start | bytes 95240 | tf_op jit(solution)/shard_map/ppermute | solution.py:12
  232.1 8.8 %collective-permute-start.1 = (f32[31,256]{1,0:T(8,128)S(1)}, f32[31,256]{1,0:T(8,128)S(1)}, u32[]{:S(2)}, u32[]{:S(2)}) collective-permute-start(f32[31,256]{1,0:T(8,128)S(1)} %collective-permute-done), channel_id=1, source_target_pairs={{1,0},{2,1},{3,2},{4,3},{5,4},{6,5},{7,6},{8,7},{9,8},{10,9},{11,1... | collective-permute-start | bytes 95240 | tf_op jit(solution)/shard_map/ppermute | solution.py:18
  385.4 149.4 %copy-start.3 = (f32[512]{0:T(512)}, f32[512]{0:T(512)S(1)}, u32[]{:S(2)}) copy-start(f32[512]{0:T(512)S(1)} %get-tuple-element.34) | copy-start | bytes 6148
Sparse Core Ops, SparseCore 0:
  386.2 147.2 all-reduce.1
